TPU v7x, 32 devices: a whole 2x2x4 slice. The times are simulated.
32 devices in a mesh: samp: 4 (over y, x), var: 8 (over z, core).
Axes of the slice: x: 2, y: 2, z: 4, core: 2. Of those that a mesh axis runs over, the one named last changes fastest.
Arguments:
- dosage: bfloat16 [8192, 16384], P('samp', 'var'), may hold values from -6 to 6
- traits: float32 [8192, 128], P(('samp', 'var')), may hold values from -6 to 6
- coef_now: float32 [128, 256, 128], P('var', 'samp'), may hold values from -6 to 6
- coef_prev: float32 [128, 256, 128], P('var', 'samp'), may hold values from -6 to 6
- block_inverse: bfloat16 [128, 256, 4, 256], P('var', 'samp'), may hold values from -0.1875 to 0.1875
- penalty: float32 [128], replicated, may hold values from 0.05 to 0.5
- block_start: int32 [64], replicated, may hold values from 0 to 1, as said below
- unit_owner: int32 [64], replicated, may hold values from 0 to 7, as said below
Outputs:
- coef_next: float32 [128, 256, 128], P('var', 'samp')
- residual: float32 [8192, 128], P(('samp', 'var'))
Inputs may be any that keep to these rules, and one draw needn't show every extreme that they name: `block_start`: 1 where a linkage block begins, else 0. The first unit of every device's 8 units begins a block, and a block holds 1 to 4 units of 256 variants. `unit_owner`: the index along var of the device that owns each unit's block, equal for all units of a block. For a unit of the device with index d along var it is (d + j) modulo the size of var, with 1 <= j <= 4. An owner holds at most 16 units and some owner holds exactly 16; the units of one device that belong to one owner are at most 4, and some device has exactly 4 for one owner.
All inputs are finite; a program needn't handle non-finite values.
Results may differ from a plain program's by a relative error of at most 0.0072.
Values may be sent and summed in bfloat16 or wider, within the bound.
No kernel may reach another device: no remote copies, remote signals or barrier semaphores. Data moves between devices by JAX's collectives and lax.ppermute only.
A program may use at most 64 MiB of HBM per device.

v0:
```python
import math
import jax
import jax.numpy as jnp
from jax import lax
from jax.sharding import PartitionSpec as P

MOMENTA = (0.4, 0.55)


def shifted(block, axis, distance):
    devices = range(lax.axis_size(axis))
    route = [((i - distance) % len(devices), i) for i in devices]
    return lax.ppermute(block, axis, route)


def unit_tables(block_start, unit_owner, per_device, owners):
    unit_count = block_start.shape[0]
    unit_ids = jnp.arange(unit_count, dtype=jnp.int32)
    shard_of = unit_ids // per_device
    owner_hot = (unit_owner[:, None] == jnp.arange(owners, dtype=jnp.int32)[None, :]).astype(
        jnp.int32
    )
    running = jnp.cumsum(owner_hot, axis=0) - owner_hot
    slot_index = jnp.sum(running * owner_hot, axis=1)
    first_unit = shard_of * per_device
    before_shard = jnp.sum(running[first_unit] * owner_hot, axis=1)
    pair_place = slot_index - before_shard
    block_begin = lax.cummax(jnp.where(block_start == 1, unit_ids, 0), axis=0)
    block_later = lax.cummin(
        jnp.where(block_start == 1, unit_ids, unit_count), axis=0, reverse=True
    )
    block_follow = jnp.concatenate([block_later[1:], jnp.full((1,), unit_count, jnp.int32)])
    block_length = block_follow - block_begin
    offset = unit_ids - block_begin
    return (shard_of, slot_index, pair_place, offset, block_length)


def shards(dosage, traits, coef_now, coef_prev, block_inverse, penalty, block_start, unit_owner):
    owners = lax.axis_size("var")
    quarters = lax.axis_size("samp")
    var_index = lax.axis_index("var")
    samp_index = lax.axis_index("samp")
    capacity = coef_now.shape[0]
    quarter_rows = coef_now.shape[1]
    right_cols = coef_now.shape[2]
    unit_rows = block_inverse.shape[3]
    block_most = block_inverse.shape[2]
    per_device = dosage.shape[1] // unit_rows
    pair_cap = min(block_most, per_device)
    reach = capacity // pair_cap
    samples = dosage.shape[0] * quarters
    variants = dosage.shape[1] * owners
    inv_scale = 1.0 / math.sqrt(variants)
    grad_scale = 0.5 / math.sqrt(samples)
    shard_of, slot_index, pair_place, offset, block_length = unit_tables(
        block_start, unit_owner, per_device, owners
    )
    owner_gap = (unit_owner - shard_of) % owners
    unit_code = (owner_gap - 1) * pair_cap + pair_place
    columns = jnp.arange(reach * pair_cap, dtype=jnp.int32)
    local_ids = var_index * per_device + jnp.arange(per_device, dtype=jnp.int32)
    local_code = unit_code[local_ids]
    matches = local_code[None, :] == columns[:, None]
    send_unit = jnp.sum(
        matches.astype(jnp.int32) * jnp.arange(per_device, dtype=jnp.int32)[None, :], axis=1
    )
    send_live = jnp.any(matches, axis=1)
    owned_flag = unit_owner == var_index
    slot_match = owned_flag[None, :] & (
        slot_index[None, :] == jnp.arange(capacity, dtype=jnp.int32)[:, None]
    )
    slot_hits = slot_match.astype(jnp.int32)
    slot_live = jnp.any(slot_match, axis=1)
    slot_code = jnp.sum(slot_hits * unit_code[None, :], axis=1)
    slot_offset = jnp.sum(slot_hits * offset[None, :], axis=1)
    slot_length = jnp.sum(slot_hits * block_length[None, :], axis=1)
    back_match = slot_live[None, :] & (slot_code[None, :] == columns[:, None])
    back_slot = jnp.sum(
        back_match.astype(jnp.int32) * jnp.arange(capacity, dtype=jnp.int32)[None, :], axis=1
    )
    back_live = jnp.any(back_match, axis=1)
    within = jnp.arange(block_most, dtype=jnp.int32)
    member_ids = jnp.clip(
        jnp.arange(capacity, dtype=jnp.int32)[:, None] - slot_offset[:, None] + within[None, :],
        0,
        capacity - 1,
    )
    member_live = (within[None, :] < slot_length[:, None]) & slot_live[:, None]
    panel_rows = block_inverse.reshape(capacity, quarter_rows, block_most * unit_rows)
    zero_half = jnp.zeros((), jnp.bfloat16)
    current, previous = (coef_now, coef_prev)
    residual = traits
    for momentum in MOMENTA:
        point = current + momentum * (current - previous)
        send_outgoing = jnp.where(
            back_live[:, None, None], point.astype(jnp.bfloat16)[back_slot], zero_half
        )
        send_outgoing = send_outgoing.reshape(reach, pair_cap, quarter_rows, right_cols)
        send_pieces = []
        for send_gap in range(1, reach + 1):
            send_pieces.append(shifted(send_outgoing[send_gap - 1], "var", -send_gap))
        send_received = jnp.stack(send_pieces).reshape(reach * pair_cap, quarter_rows, right_cols)
        local_rows = send_received[local_code]
        send_gathered = lax.all_gather(local_rows[:, None], "samp", axis=1, tiled=True)
        values = send_gathered.reshape(per_device * unit_rows, right_cols)
        summed = lax.psum_scatter(
            jnp.dot(dosage, values, preferred_element_type=jnp.float32) * inv_scale,
            "var",
            scatter_dimension=0,
            tiled=True,
        )
        residual = summed - traits
        residual_b = lax.all_gather(residual.astype(jnp.bfloat16), "var", axis=0, tiled=True)
        partial_grad = (
            lax.dot_general(
                dosage, residual_b, (((0,), (0,)), ((), ())), preferred_element_type=jnp.float32
            )
            * grad_scale
        )
        shaped = partial_grad.reshape(per_device, quarters, quarter_rows, right_cols)
        grad_sum = lax.psum(shaped, "samp")
        own_grad = lax.dynamic_index_in_dim(grad_sum, samp_index, 1, keepdims=False)
        outgoing = jnp.where(
            send_live[:, None, None], own_grad.astype(jnp.bfloat16)[send_unit], zero_half
        )
        outgoing = outgoing.reshape(reach, pair_cap, quarter_rows, right_cols)
        pieces = []
        for gap in range(1, reach + 1):
            pieces.append(shifted(outgoing[gap - 1], "var", gap))
        received = jnp.stack(pieces).reshape(reach * pair_cap, quarter_rows, right_cols)
        held_rows = jnp.where(slot_live[:, None, None], received[slot_code], zero_half)
        gathered = lax.all_gather(held_rows[:, None], "samp", axis=1, tiled=True)
        whole_grad = gathered.reshape(capacity, unit_rows, right_cols)
        block_grad = jnp.where(member_live[:, :, None, None], whole_grad[member_ids], zero_half)
        block_grad = block_grad.reshape(capacity, block_most * unit_rows, right_cols)
        direction = jnp.einsum(
            "irc,ick->irk", panel_rows, block_grad, preferred_element_type=jnp.float32
        )
        stepped = point - direction
        updated = jnp.sign(stepped) * jnp.maximum(jnp.abs(stepped) - penalty, 0.0)
        updated = jnp.where(slot_live[:, None, None], updated, jnp.float32(0.0))
        previous, current = (current, updated)
    return (current, residual)


def solution(mesh):
    placed = (
        P("samp", "var"),
        P(("samp", "var"), None),
        P("var", "samp", None),
        P("var", "samp", None),
        P("var", "samp", None, None),
        P(),
        P(),
        P(),
    )
    return jax.shard_map(
        shards,
        mesh=mesh,
        in_specs=placed,
        out_specs=(P("var", "samp", None), P(("samp", "var"), None)),
        check_vma=False,
    )
```

profile of v0, /device:TPU:0, one launch (start us, length us, event | category | flops | bytes accessed | tf_op | source)
XLA Modules:
  0.0 374.6 jit_solution(17077146969779160908)
XLA Ops:
  15.9 4.6 %collective-permute-start = (bf16[4,64,128]{2,1,0:T(8,128)(2,1)S(1)}, bf16[4,64,128]{2,1,0:T(8,128)(2,1)S(1)}, u32[]{:S(2)}, u32[]{:S(2)}) collective-permute-start(bf16[4,64,128]{2,1,0:T(8,128)(2,1)S(1)} %get-tuple-element.27), channel_id=1, source_target_pairs={{1,0},{2,1},{3,2},{4,3},{5,4},{6,5},{7,6},{0,7},{9,8},{10,9},{11,1... | collective-permute-start | bytes 196616 | tf_op jit(solution)/shard_map/ppermute | solution.py:13
  20.5 3.3 collective-permute-start.1
  24.5 2.6 collective-permute-done.3
  27.7 11.3 %all-gather = bf16[8,256,128]{2,1,0:T(8,128)(2,1)S(1)} all-gather(bf16[8,64,128]{2,1,0:T(8,128)(2,1)S(1)} %gather_fusion.3), channel_id=2, replica_groups=mesh['samp'=4,'var'=8] {'samp'}, dimensions={1}, use_global_device_ids=true | all-gather | bytes 655360 | tf_op jit(solution)/shard_map/all_gather | solution.py:104
  39.0 7.4 %fusion.3 = f32[2048,128]{0,1:T(8,128)} fusion(bf16[2048,128]{1,0:T(8,128)(2,1)S(1)} %bitcast.106, bf16[2048,2048]{1,0:T(8,128)(2,1)} %param.8), kind=kOutput, calls=%fused_computation.21 | convolution fusion | flops 1074003968 | bytes 9961472 | tf_op jit(solution)/shard_map/dot_general | solution.py:107
  46.8 32.6 %reduce-scatter.3.cloned.1.call-done = f32[256,128]{0,1:T(8,128)} async-done(((f32[2048,128]{0,1:T(8,128)}), f32[256,128]{0,1:T(8,128)}) %reduce-scatter.3.cloned.1.call-update) | async-done | bytes 131088 | tf_op jit(solution)/shard_map/reduce_scatter | solution.py:106
  80.3 14.9 %all_gather.19 = bf16[2048,128]{0,1:T(8,128)(2,1)S(1)} all-gather(bf16[256,128]{0,1:T(8,128)(2,1)S(1)} %subtract_convert_fusion), channel_id=1, replica_groups=mesh['samp'=4,'var'=8] {'var'}, dimensions={0}, use_global_device_ids=true | all-gather | bytes 589824 | tf_op jit(solution)/shard_map/all_gather | solution.py:113
  95.3 4.7 %fusion.2 = f32[2048,128]{0,1:T(8,128)S(1)} fusion(bf16[2048,128]{0,1:T(8,128)(2,1)S(1)} %all_gather.19, bf16[2048,2048]{1,0:T(8,128)(2,1)} %param.8), kind=kOutput, calls=%fused_computation.19 | convolution fusion | flops 1074003968 | bytes 9961472 | tf_op jit(solution)/shard_map/dot_general | solution.py:115
  100.3 41.9 %all-reduce.2 = bf16[8,4,64,128]{3,2,1,0:T(8,128)(2,1)S(1)} all-reduce(f32[8,4,64,128]{3,2,1,0:T(8,128)S(1)} %bitcast.104), channel_id=1, replica_groups=mesh['samp'=4,'var'=8] {'samp'}, use_global_device_ids=true, to_apply=%region_12.13 | all-reduce | flops 262144 | bytes 1572864 | tf_op jit(solution)/shard_map/psum | solution.py:121
  143.8 3.1 collective-permute-start.6
  148.6 4.5 %collective-permute-done.7 = bf16[4,64,128]{2,1,0:T(8,128)(2,1)S(1)} collective-permute-done((bf16[4,64,128]{2,1,0:T(8,128)(2,1)S(1)}, bf16[4,64,128]{2,1,0:T(8,128)(2,1)S(1)}, u32[]{:S(2)}, u32[]{:S(2)}) %collective-permute-start.7) | collective-permute-done | bytes 65568 | tf_op jit(solution)/shard_map/ppermute | solution.py:13
  155.1 3.2 reshape.362
  158.3 20.1 %all-gather.5.cloned.1.call-done = bf16[16,4,64,128]{3,2,1,0:T(8,128)(2,1)} async-done(((bf16[16,1,64,128]{3,2,1,0:T(8,128)(2,1)}), bf16[16,4,64,128]{3,2,1,0:T(8,128)(2,1)}) %all-gather.5.cloned.1.call-update) | async-done | bytes 1048592 | tf_op jit(solution)/shard_map/all_gather | solution.py:132
  178.5 4.2 %gather_fusion.6 = bf16[64,256,128]{2,1,0:T(8,128)(2,1)} fusion(bf16[16,256,128]{2,1,0:T(8,128)(2,1)} %bitcast.100, s32[1024]{0:T(1024)S(1)} %pad_clamp_fusion), kind=kCustom, calls=%fused_computation.6 | custom fusion | bytes 8388864 | tf_op jit(solution)/shard_map/gather | solution.py:134
  182.7 6.2 %bitcast_select_fusion.1 = bf16[16,1024,128]{2,1,0:T(8,128)(2,1)S(1)} fusion(pred[16,1024]{1,0:T(8,128)(4,1)S(1)} %bitcast.112, bf16[16,1024,128]{2,1,0:T(8,128)(2,1)} %bitcast.103), kind=kLoop, calls=%fused_computation.13 | loop fusion | flops 2097152 | bytes 8404992 | tf_op jit(solution)/shard_map/jit(_where)/select_n | solution.py:134
  188.9 1.8 fusion.36
  191.5 2.7 collective-permute-start.8
  194.3 3.3 collective-permute-start.9
  197.6 3.1 collective-permute-done.11
  201.3 11.5 %all-gather.1 = bf16[8,256,128]{2,1,0:T(8,128)(2,1)S(1)} all-gather(bf16[8,64,128]{2,1,0:T(8,128)(2,1)S(1)} %gather_fusion.8), channel_id=3, replica_groups=mesh['samp'=4,'var'=8] {'samp'}, dimensions={1}, use_global_device_ids=true | all-gather | bytes 655360 | tf_op jit(solution)/shard_map/all_gather | solution.py:104
  212.9 7.3 %fusion.1 = f32[2048,128]{0,1:T(8,128)} fusion(bf16[2048,128]{1,0:T(8,128)(2,1)S(1)} %bitcast.107, bf16[2048,2048]{1,0:T(8,128)(2,1)} %param.8), kind=kOutput, calls=%fused_computation.17 | convolution fusion | flops 1074003968 | bytes 9961472 | tf_op jit(solution)/shard_map/dot_general | solution.py:107
  220.2 33.1 %reduce-scatter.5.cloned.1.call-done = f32[256,128]{0,1:T(8,128)} async-done(((f32[2048,128]{0,1:T(8,128)}), f32[256,128]{0,1:T(8,128)}) %reduce-scatter.5.cloned.1.call-update) | async-done | bytes 131088 | tf_op jit(solution)/shard_map/reduce_scatter | solution.py:106
  254.2 14.9 %all_gather.22 = bf16[2048,128]{0,1:T(8,128)(2,1)S(1)} all-gather(bf16[256,128]{0,1:T(8,128)(2,1)S(1)} %get-tuple-element.13), channel_id=1, replica_groups=mesh['samp'=4,'var'=8] {'var'}, dimensions={0}, use_global_device_ids=true | all-gather | bytes 589824 | tf_op jit(solution)/shard_map/all_gather | solution.py:113
  269.2 5.7 %fusion = f32[2048,128]{0,1:T(8,128)} fusion(bf16[2048,128]{0,1:T(8,128)(2,1)S(1)} %all_gather.22, bf16[2048,2048]{1,0:T(8,128)(2,1)} %param.8), kind=kOutput, calls=%fused_computation.15 | convolution fusion | flops 1074003968 | bytes 9961472 | tf_op jit(solution)/shard_map/dot_general | solution.py:115
  276.4 42.3 %all-reduce.3 = bf16[8,4,64,128]{3,2,1,0:T(8,128)(2,1)} all-reduce(f32[8,4,64,128]{3,2,1,0:T(8,128)S(1)} %bitcast.105), channel_id=1, replica_groups=mesh['samp'=4,'var'=8] {'samp'}, use_global_device_ids=true, to_apply=%region_16.17 | all-reduce | flops 262144 | bytes 1572864 | tf_op jit(solution)/shard_map/psum | solution.py:121
  321.2 3.1 collective-permute-start.14
  324.3 1.8 collective-permute-done.12
  326.0 4.5 %collective-permute-done.15 = bf16[4,64,128]{2,1,0:T(8,128)(2,1)S(1)} collective-permute-done((bf16[4,64,128]{2,1,0:T(8,128)(2,1)S(1)}, bf16[4,64,128]{2,1,0:T(8,128)(2,1)S(1)}, u32[]{:S(2)}, u32[]{:S(2)}) %collective-permute-start.15) | collective-permute-done | bytes 65568 | tf_op jit(solution)/shard_map/ppermute | solution.py:13
  332.8 23.1 %all-gather.7.cloned.1.call-done = bf16[16,4,64,128]{3,2,1,0:T(8,128)(2,1)} async-done(((bf16[16,1,64,128]{3,2,1,0:T(8,128)(2,1)}), bf16[16,4,64,128]{3,2,1,0:T(8,128)(2,1)}) %all-gather.7.cloned.1.call-update) | async-done | bytes 1048592 | tf_op jit(solution)/shard_map/all_gather | solution.py:132
  355.9 4.2 %gather_fusion.11 = bf16[64,256,128]{2,1,0:T(8,128)(2,1)} fusion(bf16[16,256,128]{2,1,0:T(8,128)(2,1)} %bitcast.101, s32[1024]{0:T(1024)S(1)} %pad_clamp_fusion), kind=kCustom, calls=%fused_computation.11 | custom fusion | bytes 8388864 | tf_op jit(solution)/shard_map/gather | solution.py:134
  360.1 6.1 %bitcast_select_fusion = bf16[16,1024,128]{2,1,0:T(8,128)(2,1)S(1)} fusion(pred[16,1024]{1,0:T(8,128)(4,1)S(1)} %bitcast.113, bf16[16,1024,128]{2,1,0:T(8,128)(2,1)} %bitcast.102), kind=kLoop, calls=%fused_computation.12 | loop fusion | flops 2097152 | bytes 8404992 | tf_op jit(solution)/shard_map/jit(_where)/select_n | solution.py:134
  366.3 1.8 multiply_select_fusion
  (110 shorter events, 25.4 us)
Async XLA Ops:
  7.2 72.2 %reduce-scatter.3.cloned.1.call-start = ((), (), s32[]{:S(2)}) async-start(), calls=%async_computation.2 | async-start | bytes 1179648 | tf_op jit(solution)/shard_map/reduce_scatter | solution.py:106
  15.9 8.6 %collective-permute-start = (bf16[4,64,128]{2,1,0:T(8,128)(2,1)S(1)}, bf16[4,64,128]{2,1,0:T(8,128)(2,1)S(1)}, u32[]{:S(2)}, u32[]{:S(2)}) collective-permute-start(bf16[4,64,128]{2,1,0:T(8,128)(2,1)S(1)} %get-tuple-element.27), channel_id=1, source_target_pairs={{1,0},{2,1},{3,2},{4,3},{5,4},{6,5},{7,6},{0,7},{9,8},{10,9},{11,1... | collective-permute-start | bytes 196616 | tf_op jit(solution)/shard_map/ppermute | solution.py:13
  20.5 6.6 %collective-permute-start.3 = (bf16[4,64,128]{2,1,0:T(8,128)(2,1)S(1)}, bf16[4,64,128]{2,1,0:T(8,128)(2,1)S(1)}, u32[]{:S(2)}, u32[]{:S(2)}) collective-permute-start(bf16[4,64,128]{2,1,0:T(8,128)(2,1)S(1)} %get-tuple-element.28), channel_id=1, source_target_pairs={{4,0},{5,1},{6,2},{7,3},{0,4},{1,5},{2,6},{3,7},{12,8},{13,9},{14,... | collective-permute-start | bytes 196616 | tf_op jit(solution)/shard_map/ppermute | solution.py:13
  20.5 6.6 %collective-permute-start.2 = (bf16[4,64,128]{2,1,0:T(8,128)(2,1)S(1)}, bf16[4,64,128]{2,1,0:T(8,128)(2,1)S(1)}, u32[]{:S(2)}, u32[]{:S(2)}) collective-permute-start(bf16[4,64,128]{2,1,0:T(8,128)(2,1)S(1)} %get-tuple-element.29), channel_id=1, source_target_pairs={{3,0},{4,1},{5,2},{6,3},{7,4},{0,5},{1,6},{2,7},{11,8},{12,9},{13,... | collective-permute-start | bytes 196616 | tf_op jit(solution)/shard_map/ppermute | solution.py:13
  20.5 6.6 %collective-permute-start.1 = (bf16[4,64,128]{2,1,0:T(8,128)(2,1)S(1)}, bf16[4,64,128]{2,1,0:T(8,128)(2,1)S(1)}, u32[]{:S(2)}, u32[]{:S(2)}) collective-permute-start(bf16[4,64,128]{2,1,0:T(8,128)(2,1)S(1)} %get-tuple-element.30), channel_id=1, source_target_pairs={{2,0},{3,1},{4,2},{5,3},{6,4},{7,5},{0,6},{1,7},{10,8},{11,9},{12,... | collective-permute-start | bytes 196616 | tf_op jit(solution)/shard_map/ppermute | solution.py:13
  39.0 7.4 %copy-start.3 = (f32[256,128]{1,0:T(8,128)S(1)}, f32[256,128]{1,0:T(8,128)}, u32[]{:S(2)}) copy-start(f32[256,128]{1,0:T(8,128)} %param.9) | copy-start | bytes 393220
  46.4 132.1 %all-gather.5.cloned.1.call-start = ((), (), s32[]{:S(2)}) async-start(), calls=%async_computation.3 | async-start | bytes 1310720 | tf_op jit(solution)/shard_map/all_gather | solution.py:132
  143.0 5.6 %collective-permute-start.4 = (bf16[4,64,128]{2,1,0:T(8,128)(2,1)S(1)}, bf16[4,64,128]{2,1,0:T(8,128)(2,1)S(1)}, u32[]{:S(2)}, u32[]{:S(2)}) collective-permute-start(bf16[4,64,128]{2,1,0:T(8,128)(2,1)S(1)} %get-tuple-element.23), channel_id=1, source_target_pairs={{7,0},{0,1},{1,2},{2,3},{3,4},{4,5},{5,6},{6,7},{15,8},{8,9},{9,10... | collective-permute-start | bytes 196616 | tf_op jit(solution)/shard_map/ppermute | solution.py:13
  143.1 10.1 %collective-permute-start.7 = (bf16[4,64,128]{2,1,0:T(8,128)(2,1)S(1)}, bf16[4,64,128]{2,1,0:T(8,128)(2,1)S(1)}, u32[]{:S(2)}, u32[]{:S(2)}) collective-permute-start(bf16[4,64,128]{2,1,0:T(8,128)(2,1)S(1)} %get-tuple-element.24), channel_id=1, source_target_pairs={{4,0},{5,1},{6,2},{7,3},{0,4},{1,5},{2,6},{3,7},{12,8},{13,9},{14,... | collective-permute-start | bytes 196616 | tf_op jit(solution)/shard_map/ppermute | solution.py:13
  143.8 9.4 %collective-permute-start.6 = (bf16[4,64,128]{2,1,0:T(8,128)(2,1)S(1)}, bf16[4,64,128]{2,1,0:T(8,128)(2,1)S(1)}, u32[]{:S(2)}, u32[]{:S(2)}) collective-permute-start(bf16[4,64,128]{2,1,0:T(8,128)(2,1)S(1)} %get-tuple-element.25), channel_id=1, source_target_pairs={{5,0},{6,1},{7,2},{0,3},{1,4},{2,5},{3,6},{4,7},{13,8},{14,9},{15,... | collective-permute-start | bytes 196616 | tf_op jit(solution)/shard_map/ppermute | solution.py:13
  146.9 6.3 %collective-permute-start.5 = (bf16[4,64,128]{2,1,0:T(8,128)(2,1)S(1)}, bf16[4,64,128]{2,1,0:T(8,128)(2,1)S(1)}, u32[]{:S(2)}, u32[]{:S(2)}) collective-permute-start(bf16[4,64,128]{2,1,0:T(8,128)(2,1)S(1)} %get-tuple-element.26), channel_id=1, source_target_pairs={{6,0},{7,1},{0,2},{1,3},{2,4},{3,5},{4,6},{5,7},{14,8},{15,9},{8,1... | collective-permute-start | bytes 196616 | tf_op jit(solution)/shard_map/ppermute | solution.py:13
  154.7 98.7 %reduce-scatter.5.cloned.1.call-start = ((), (), s32[]{:S(2)}) async-start(), calls=%async_computation.4 | async-start | bytes 1179648 | tf_op jit(solution)/shard_map/reduce_scatter | solution.py:106
  182.7 6.2 %copy-start = (f32[16,64,128]{2,1,0:T(8,128)S(1)}, f32[16,64,128]{2,1,0:T(8,128)}, u32[]{:S(2)}) copy-start(f32[16,64,128]{2,1,0:T(8,128)} %param.10) | copy-start | bytes 1572868
  182.7 6.2 %copy-start.1 = (f32[16,64,128]{2,1,0:T(8,128)S(1)}, f32[16,64,128]{2,1,0:T(8,128)}, u32[]{:S(2)}) copy-start(f32[16,64,128]{2,1,0:T(8,128)} %param.11) | copy-start | bytes 1572868
  182.7 6.2 %copy-start.4 = (f32[128]{0:T(128)S(1)}, f32[128]{0:T(128)}, u32[]{:S(2)}) copy-start(f32[128]{0:T(128)} %param.13) | copy-start | bytes 1540
  191.5 6.1 %collective-permute-start.8 = (bf16[4,64,128]{2,1,0:T(8,128)(2,1)S(1)}, bf16[4,64,128]{2,1,0:T(8,128)(2,1)S(1)}, u32[]{:S(2)}, u32[]{:S(2)}) collective-permute-start(bf16[4,64,128]{2,1,0:T(8,128)(2,1)S(1)} %get-tuple-element.19), channel_id=1, source_target_pairs={{1,0},{2,1},{3,2},{4,3},{5,4},{6,5},{7,6},{0,7},{9,8},{10,9},{11,1... | collective-permute-start | bytes 196616 | tf_op jit(solution)/shard_map/ppermute | solution.py:13
  194.1 6.6 %collective-permute-start.11 = (bf16[4,64,128]{2,1,0:T(8,128)(2,1)S(1)}, bf16[4,64,128]{2,1,0:T(8,128)(2,1)S(1)}, u32[]{:S(2)}, u32[]{:S(2)}) collective-permute-start(bf16[4,64,128]{2,1,0:T(8,128)(2,1)S(1)} %get-tuple-element.20), channel_id=1, source_target_pairs={{4,0},{5,1},{6,2},{7,3},{0,4},{1,5},{2,6},{3,7},{12,8},{13,9},{14,... | collective-permute-start | bytes 196616 | tf_op jit(solution)/shard_map/ppermute | solution.py:13
  194.1 6.6 %collective-permute-start.10 = (bf16[4,64,128]{2,1,0:T(8,128)(2,1)S(1)}, bf16[4,64,128]{2,1,0:T(8,128)(2,1)S(1)}, u32[]{:S(2)}, u32[]{:S(2)}) collective-permute-start(bf16[4,64,128]{2,1,0:T(8,128)(2,1)S(1)} %get-tuple-element.21), channel_id=1, source_target_pairs={{3,0},{4,1},{5,2},{6,3},{7,4},{0,5},{1,6},{2,7},{11,8},{12,9},{13,... | collective-permute-start | bytes 196616 | tf_op jit(solution)/shard_map/ppermute | solution.py:13
  194.3 6.4 %collective-permute-start.9 = (bf16[4,64,128]{2,1,0:T(8,128)(2,1)S(1)}, bf16[4,64,128]{2,1,0:T(8,128)(2,1)S(1)}, u32[]{:S(2)}, u32[]{:S(2)}) collective-permute-start(bf16[4,64,128]{2,1,0:T(8,128)(2,1)S(1)} %get-tuple-element.22), channel_id=1, source_target_pairs={{2,0},{3,1},{4,2},{5,3},{6,4},{7,5},{0,6},{1,7},{10,8},{11,9},{12,... | collective-permute-start | bytes 196616 | tf_op jit(solution)/shard_map/ppermute | solution.py:13
  220.2 135.7 %all-gather.7.cloned.1.call-start = ((), (), s32[]{:S(2)}) async-start(), calls=%async_computation.5 | async-start | bytes 1310720 | tf_op jit(solution)/shard_map/all_gather | solution.py:132
  320.4 5.6 %collective-permute-start.12 = (bf16[4,64,128]{2,1,0:T(8,128)(2,1)S(1)}, bf16[4,64,128]{2,1,0:T(8,128)(2,1)S(1)}, u32[]{:S(2)}, u32[]{:S(2)}) collective-permute-start(bf16[4,64,128]{2,1,0:T(8,128)(2,1)S(1)} %get-tuple-element.15), channel_id=1, source_target_pairs={{7,0},{0,1},{1,2},{2,3},{3,4},{4,5},{5,6},{6,7},{15,8},{8,9},{9,10... | collective-permute-start | bytes 196616 | tf_op jit(solution)/shard_map/ppermute | solution.py:13
  320.5 10.1 %collective-permute-start.15 = (bf16[4,64,128]{2,1,0:T(8,128)(2,1)S(1)}, bf16[4,64,128]{2,1,0:T(8,128)(2,1)S(1)}, u32[]{:S(2)}, u32[]{:S(2)}) collective-permute-start(bf16[4,64,128]{2,1,0:T(8,128)(2,1)S(1)} %get-tuple-element.16), channel_id=1, source_target_pairs={{4,0},{5,1},{6,2},{7,3},{0,4},{1,5},{2,6},{3,7},{12,8},{13,9},{14,... | collective-permute-start | bytes 196616 | tf_op jit(solution)/shard_map/ppermute | solution.py:13
  321.2 9.4 %collective-permute-start.14 = (bf16[4,64,128]{2,1,0:T(8,128)(2,1)S(1)}, bf16[4,64,128]{2,1,0:T(8,128)(2,1)S(1)}, u32[]{:S(2)}, u32[]{:S(2)}) collective-permute-start(bf16[4,64,128]{2,1,0:T(8,128)(2,1)S(1)} %get-tuple-element.17), channel_id=1, source_target_pairs={{5,0},{6,1},{7,2},{0,3},{1,4},{2,5},{3,6},{4,7},{13,8},{14,9},{15,... | collective-permute-start | bytes 196616 | tf_op jit(solution)/shard_map/ppermute | solution.py:13
  324.3 6.3 %collective-permute-start.13 = (bf16[4,64,128]{2,1,0:T(8,128)(2,1)S(1)}, bf16[4,64,128]{2,1,0:T(8,128)(2,1)S(1)}, u32[]{:S(2)}, u32[]{:S(2)}) collective-permute-start(bf16[4,64,128]{2,1,0:T(8,128)(2,1)S(1)} %get-tuple-element.18), channel_id=1, source_target_pairs={{6,0},{7,1},{0,2},{1,3},{2,4},{3,5},{4,6},{5,7},{14,8},{15,9},{8,1... | collective-permute-start | bytes 196616 | tf_op jit(solution)/shard_map/ppermute | solution.py:13
  360.1 6.1 %copy-start.2 = (f32[16,64,128]{2,1,0:T(8,128)S(1)}, f32[16,64,128]{2,1,0:T(8,128)}, u32[]{:S(2)}) copy-start(f32[16,64,128]{2,1,0:T(8,128)} %get-tuple-element.36) | copy-start | bytes 1572868
Sparse Core Ops, SparseCore 0:
  46.5 32.8 reduce-scatter.2
  154.8 23.6 all-gather.4
  220.3 32.9 reduce-scatter.4
  332.2 23.6 all-gather.6
where the time goes:
time: 375 us
  blocking collectives  137 us (37%)
  waiting for transfers between devices  127 us (34%)
  matrix products  28.7 us (8%)
  other arithmetic  23.6 us (6%)
  starting transfers between devices  21.9 us (6%)
  local copies, waits for them, and re-layouts  21.9 us (6%)
  between operations  14.2 us (4%)
    psum x2, blocking collectives, shards(): grad_sum = lax.psum(shaped, 'samp')  84.2 us
    reduce_scatter x2, waiting for transfers between devices, shards(): lax.psum_scatter(jnp.dot(dosage, values, preferred_element_type=jnp.float...  65.7 us
    all_gather x2, waiting for transfers between devices, shards(): gathered = lax.all_gather(held_rows[:, None], 'samp', axis=1, tiled=True)  43.2 us
    all_gather x2, blocking collectives, shards(): lax.all_gather(residual.astype(jnp.bfloat16), 'var', axis=0, tiled=True)  29.9 us
    all_gather x2, blocking collectives, shards(): lax.all_gather(local_rows[:, None], 'samp', axis=1, tiled=True)  22.8 us
    ppermute x16, starting transfers between devices, shifted(): return lax.ppermute(block, axis, route)  21.8 us
    ppermute x16, waiting for transfers between devices, shifted(): return lax.ppermute(block, axis, route)  18.3 us
    dot_general x2, matrix products, shards(): jnp.dot(dosage, values, preferred_element_type=jnp.float32) * inv_scale  14.7 us
  transfers between devices with their start and end apart: 20, of which 12 were waited for; matrix products, arithmetic and copies ran while one was open for 1% of the time, Pallas kernels for 0%

commit v1 on v0

--- a/solution.py
+++ b/solution.py
@@ -1,3 +1,4 @@
+import functools
 import math
 import jax
 import jax.numpy as jnp
@@ -5,6 +6,17 @@
 from jax.sharding import PartitionSpec as P
 
 MOMENTA = (0.4, 0.55)
+
+
+def _get_seats_all(inp, dev_axis):
+    axis_len = jax.lax.axis_size(dev_axis)
+    n_now = inp
+    for kk in [[(j, j ^ i0) for j in range(axis_len)] for i0 in (1, 2, 4, 8, 16) if i0 < axis_len]:
+        n_now = n_now + jax.lax.ppermute(n_now, dev_axis, kk)
+    return n_now
+
+
+treat_figure = functools.partial(_get_seats_all, dev_axis="samp")
 
 
 def shifted(block, axis, distance):
@@ -118,7 +130,7 @@
             * grad_scale
         )
         shaped = partial_grad.reshape(per_device, quarters, quarter_rows, right_cols)
-        grad_sum = lax.psum(shaped, "samp")
+        grad_sum = treat_figure(shaped)
         own_grad = lax.dynamic_index_in_dim(grad_sum, samp_index, 1, keepdims=False)
         outgoing = jnp.where(
             send_live[:, None, None], own_grad.astype(jnp.bfloat16)[send_unit], zero_half

time: 375 us -> 393 us (1.048)
  waiting for transfers between devices: 127 us -> 224 us
  blocking collectives: 137 us -> 52.8 us
  starting transfers between devices: 21.9 us -> 28 us
    ppermute x0 -> x4, waiting for transfers between devices: none -> 93.9 us  [_get_seats_all(): n_now = n_now + jax.lax.ppermute(n_now, dev_axis, kk)]
    psum x2 -> x0, blocking collectives: 84.2 us -> none  [shards(): grad_sum = lax.psum(shaped, 'samp')]
    ppermute x0 -> x4, starting transfers between devices: none -> 6.07 us  [_get_seats_all(): n_now = n_now + jax.lax.ppermute(n_now, dev_axis, kk)]
  transfers between devices with their start and end apart: 20 -> 24, of which waited for: 12 -> 16; matrix products, arithmetic and copies ran while one was open for 1% -> 1% of each run, Pallas kernels for 0% -> 0%
where the time goes in v1:
time: 393 us; the launch traced here: 392 us
  waiting for transfers between devices  224 us (57%)
  blocking collectives  52.8 us (13%)
  matrix products  28.6 us (7%)
  starting transfers between devices  28 us (7%)
  other arithmetic  24.1 us (6%)
  local copies, waits for them, and re-layouts  21 us (5%)
  between operations  14.2 us (4%)
    ppermute x4, waiting for transfers between devices, _get_seats_all(): n_now = n_now + jax.lax.ppermute(n_now, dev_axis, kk)  93.9 us
    reduce_scatter x2, waiting for transfers between devices, shards(): lax.psum_scatter(jnp.dot(dosage, values, preferred_element_type=jnp.float...  65.9 us
    all_gather x2, waiting for transfers between devices, shards(): gathered = lax.all_gather(held_rows[:, None], 'samp', axis=1, tiled=True)  45.4 us
    all_gather x2, blocking collectives, shards(): lax.all_gather(residual.astype(jnp.bfloat16), 'var', axis=0, tiled=True)  29.9 us
    all_gather x2, blocking collectives, shards(): lax.all_gather(local_rows[:, None], 'samp', axis=1, tiled=True)  22.9 us
    ppermute x16, starting transfers between devices, shifted(): return lax.ppermute(block, axis, route)  21.8 us
    ppermute x16, waiting for transfers between devices, shifted(): return lax.ppermute(block, axis, route)  18.3 us
    dot_general x2, matrix products, shards(): jnp.dot(dosage, values, preferred_element_type=jnp.float32) * inv_scale  14.7 us
  transfers between devices with their start and end apart: 24, of which 16 were waited for; matrix products, arithmetic and copies ran while one was open for 1% of the time, Pallas kernels for 0%

profile of v1, /device:TPU:0, one launch (start us, length us, event | category | flops | bytes accessed | tf_op | source)
XLA Modules:
  0.0 392.2 jit_solution(11516396567861290635)
XLA Ops:
  15.9 4.6 %collective-permute-start = (bf16[4,64,128]{2,1,0:T(8,128)(2,1)S(1)}, bf16[4,64,128]{2,1,0:T(8,128)(2,1)S(1)}, u32[]{:S(2)}, u32[]{:S(2)}) collective-permute-start(bf16[4,64,128]{2,1,0:T(8,128)(2,1)S(1)} %get-tuple-element.27), channel_id=1, source_target_pairs={{1,0},{2,1},{3,2},{4,3},{5,4},{6,5},{7,6},{0,7},{9,8},{10,9},{11,1... | collective-permute-start | bytes 196616 | tf_op jit(solution)/shard_map/ppermute | solution.py:25
  20.5 3.3 collective-permute-start.1
  24.5 2.6 collective-permute-done.3
  27.7 11.3 %all-gather = bf16[8,256,128]{2,1,0:T(8,128)(2,1)S(1)} all-gather(bf16[8,64,128]{2,1,0:T(8,128)(2,1)S(1)} %gather_fusion.3), channel_id=2, replica_groups=mesh['samp'=4,'var'=8] {'samp'}, dimensions={1}, use_global_device_ids=true | all-gather | bytes 655360 | tf_op jit(solution)/shard_map/all_gather | solution.py:116
  39.0 7.4 %fusion.3 = f32[2048,128]{0,1:T(8,128)} fusion(bf16[2048,128]{1,0:T(8,128)(2,1)S(1)} %bitcast.108, bf16[2048,2048]{1,0:T(8,128)(2,1)} %param.8), kind=kOutput, calls=%fused_computation.21 | convolution fusion | flops 1074003968 | bytes 9961472 | tf_op jit(solution)/shard_map/dot_general | solution.py:119
  46.6 32.8 %reduce-scatter.3.cloned.1.call-done = f32[256,128]{0,1:T(8,128)} async-done(((f32[2048,128]{0,1:T(8,128)}), f32[256,128]{0,1:T(8,128)}) %reduce-scatter.3.cloned.1.call-update) | async-done | bytes 131088 | tf_op jit(solution)/shard_map/reduce_scatter | solution.py:118
  80.3 14.9 %all_gather.19 = bf16[2048,128]{0,1:T(8,128)(2,1)S(1)} all-gather(bf16[256,128]{0,1:T(8,128)(2,1)S(1)} %subtract_convert_fusion), channel_id=1, replica_groups=mesh['samp'=4,'var'=8] {'var'}, dimensions={0}, use_global_device_ids=true | all-gather | bytes 589824 | tf_op jit(solution)/shard_map/all_gather | solution.py:125
  95.3 4.7 %fusion.2 = f32[2048,128]{0,1:T(8,128)S(1)} fusion(bf16[2048,128]{0,1:T(8,128)(2,1)S(1)} %all_gather.19, bf16[2048,2048]{1,0:T(8,128)(2,1)} %param.8), kind=kOutput, calls=%fused_computation.19 | convolution fusion | flops 1074003968 | bytes 9961472 | tf_op jit(solution)/shard_map/dot_general | solution.py:127
  101.8 24.0 %collective-permute-done.4 = f32[8,4,64,128]{3,2,1,0:T(8,128)S(1)} collective-permute-done((f32[8,4,64,128]{3,2,1,0:T(8,128)S(1)}, f32[8,4,64,128]{3,2,1,0:T(8,128)S(1)}, u32[]{:S(2)}, u32[]{:S(2)}) %collective-permute-start.4) | collective-permute-done | bytes 1048608 | tf_op jit(solution)/shard_map/ppermute | solution.py:15
  127.7 22.9 %collective-permute-done.5 = f32[8,4,64,128]{3,2,1,0:T(8,128)S(1)} collective-permute-done((f32[8,4,64,128]{3,2,1,0:T(8,128)S(1)}, f32[8,4,64,128]{3,2,1,0:T(8,128)S(1)}, u32[]{:S(2)}, u32[]{:S(2)}) %collective-permute-start.5) | collective-permute-done | bytes 1048608 | tf_op jit(solution)/shard_map/ppermute | solution.py:15
  152.1 3.1 collective-permute-start.8
  157.0 4.5 %collective-permute-done.9 = bf16[4,64,128]{2,1,0:T(8,128)(2,1)S(1)} collective-permute-done((bf16[4,64,128]{2,1,0:T(8,128)(2,1)S(1)}, bf16[4,64,128]{2,1,0:T(8,128)(2,1)S(1)}, u32[]{:S(2)}, u32[]{:S(2)}) %collective-permute-start.9) | collective-permute-done | bytes 65568 | tf_op jit(solution)/shard_map/ppermute | solution.py:25
  163.4 3.2 reshape.362
  166.7 21.2 %all-gather.5.cloned.1.call-done = bf16[16,4,64,128]{3,2,1,0:T(8,128)(2,1)} async-done(((bf16[16,1,64,128]{3,2,1,0:T(8,128)(2,1)}), bf16[16,4,64,128]{3,2,1,0:T(8,128)(2,1)}) %all-gather.5.cloned.1.call-update) | async-done | bytes 1048592 | tf_op jit(solution)/shard_map/all_gather | solution.py:144
  188.0 4.2 %gather_fusion.6 = bf16[64,256,128]{2,1,0:T(8,128)(2,1)} fusion(bf16[16,256,128]{2,1,0:T(8,128)(2,1)} %bitcast.100, s32[1024]{0:T(1024)S(1)} %pad_clamp_fusion), kind=kCustom, calls=%fused_computation.6 | custom fusion | bytes 8388864 | tf_op jit(solution)/shard_map/gather | solution.py:146
  192.2 6.2 %bitcast_select_fusion.1 = bf16[16,1024,128]{2,1,0:T(8,128)(2,1)S(1)} fusion(pred[16,1024]{1,0:T(8,128)(4,1)S(1)} %bitcast.114, bf16[16,1024,128]{2,1,0:T(8,128)(2,1)} %bitcast.103), kind=kLoop, calls=%fused_computation.13 | loop fusion | flops 2097152 | bytes 8404992 | tf_op jit(solution)/shard_map/jit(_where)/select_n | solution.py:146
  198.4 1.8 fusion.38
  200.9 2.7 collective-permute-start.10
  203.8 3.3 collective-permute-start.11
  207.1 3.1 collective-permute-done.13
  210.8 11.6 %all-gather.1 = bf16[8,256,128]{2,1,0:T(8,128)(2,1)S(1)} all-gather(bf16[8,64,128]{2,1,0:T(8,128)(2,1)S(1)} %gather_fusion.8), channel_id=3, replica_groups=mesh['samp'=4,'var'=8] {'samp'}, dimensions={1}, use_global_device_ids=true | all-gather | bytes 655360 | tf_op jit(solution)/shard_map/all_gather | solution.py:116
  222.3 7.3 %fusion.1 = f32[2048,128]{0,1:T(8,128)} fusion(bf16[2048,128]{1,0:T(8,128)(2,1)S(1)} %bitcast.109, bf16[2048,2048]{1,0:T(8,128)(2,1)} %param.8), kind=kOutput, calls=%fused_computation.17 | convolution fusion | flops 1074003968 | bytes 9961472 | tf_op jit(solution)/shard_map/dot_general | solution.py:119
  229.7 33.1 %reduce-scatter.5.cloned.1.call-done = f32[256,128]{0,1:T(8,128)} async-done(((f32[2048,128]{0,1:T(8,128)}), f32[256,128]{0,1:T(8,128)}) %reduce-scatter.5.cloned.1.call-update) | async-done | bytes 131088 | tf_op jit(solution)/shard_map/reduce_scatter | solution.py:118
  263.7 14.9 %all_gather.22 = bf16[2048,128]{0,1:T(8,128)(2,1)S(1)} all-gather(bf16[256,128]{0,1:T(8,128)(2,1)S(1)} %get-tuple-element.13), channel_id=1, replica_groups=mesh['samp'=4,'var'=8] {'var'}, dimensions={0}, use_global_device_ids=true | all-gather | bytes 589824 | tf_op jit(solution)/shard_map/all_gather | solution.py:125
  278.7 5.7 %fusion = f32[2048,128]{0,1:T(8,128)} fusion(bf16[2048,128]{0,1:T(8,128)(2,1)S(1)} %all_gather.22, bf16[2048,2048]{1,0:T(8,128)(2,1)} %param.8), kind=kOutput, calls=%fused_computation.15 | convolution fusion | flops 1074003968 | bytes 9961472 | tf_op jit(solution)/shard_map/dot_general | solution.py:127
  287.5 23.9 %collective-permute-done.14 = f32[8,4,64,128]{3,2,1,0:T(8,128)S(1)} collective-permute-done((f32[8,4,64,128]{3,2,1,0:T(8,128)S(1)}, f32[8,4,64,128]{3,2,1,0:T(8,128)S(1)}, u32[]{:S(2)}, u32[]{:S(2)}) %collective-permute-start.14) | collective-permute-done | bytes 1048608 | tf_op jit(solution)/shard_map/ppermute | solution.py:15
  313.1 23.1 %collective-permute-done.15 = f32[8,4,64,128]{3,2,1,0:T(8,128)S(1)} collective-permute-done((f32[8,4,64,128]{3,2,1,0:T(8,128)S(1)}, f32[8,4,64,128]{3,2,1,0:T(8,128)S(1)}, u32[]{:S(2)}, u32[]{:S(2)}) %collective-permute-start.15) | collective-permute-done | bytes 1048608 | tf_op jit(solution)/shard_map/ppermute | solution.py:15
  337.7 3.1 collective-permute-start.18
  342.6 4.5 %collective-permute-done.19 = bf16[4,64,128]{2,1,0:T(8,128)(2,1)S(1)} collective-permute-done((bf16[4,64,128]{2,1,0:T(8,128)(2,1)S(1)}, bf16[4,64,128]{2,1,0:T(8,128)(2,1)S(1)}, u32[]{:S(2)}, u32[]{:S(2)}) %collective-permute-start.19) | collective-permute-done | bytes 65568 | tf_op jit(solution)/shard_map/ppermute | solution.py:25
  349.4 24.1 %all-gather.7.cloned.1.call-done = bf16[16,4,64,128]{3,2,1,0:T(8,128)(2,1)} async-done(((bf16[16,1,64,128]{3,2,1,0:T(8,128)(2,1)}), bf16[16,4,64,128]{3,2,1,0:T(8,128)(2,1)}) %all-gather.7.cloned.1.call-update) | async-done | bytes 1048592 | tf_op jit(solution)/shard_map/all_gather | solution.py:144
  373.5 4.2 %gather_fusion.11 = bf16[64,256,128]{2,1,0:T(8,128)(2,1)} fusion(bf16[16,256,128]{2,1,0:T(8,128)(2,1)} %bitcast.101, s32[1024]{0:T(1024)S(1)} %pad_clamp_fusion), kind=kCustom, calls=%fused_computation.11 | custom fusion | bytes 8388864 | tf_op jit(solution)/shard_map/gather | solution.py:146
  377.7 6.1 %bitcast_select_fusion = bf16[16,1024,128]{2,1,0:T(8,128)(2,1)S(1)} fusion(pred[16,1024]{1,0:T(8,128)(4,1)S(1)} %bitcast.115, bf16[16,1024,128]{2,1,0:T(8,128)(2,1)} %bitcast.102), kind=kLoop, calls=%fused_computation.12 | loop fusion | flops 2097152 | bytes 8404992 | tf_op jit(solution)/shard_map/jit(_where)/select_n | solution.py:146
  (118 shorter events, 34.5 us)
Async XLA Ops:
  7.2 72.2 %reduce-scatter.3.cloned.1.call-start = ((), (), s32[]{:S(2)}) async-start(), calls=%async_computation.2 | async-start | bytes 1179648 | tf_op jit(solution)/shard_map/reduce_scatter | solution.py:118
  15.9 8.6 %collective-permute-start = (bf16[4,64,128]{2,1,0:T(8,128)(2,1)S(1)}, bf16[4,64,128]{2,1,0:T(8,128)(2,1)S(1)}, u32[]{:S(2)}, u32[]{:S(2)}) collective-permute-start(bf16[4,64,128]{2,1,0:T(8,128)(2,1)S(1)} %get-tuple-element.27), channel_id=1, source_target_pairs={{1,0},{2,1},{3,2},{4,3},{5,4},{6,5},{7,6},{0,7},{9,8},{10,9},{11,1... | collective-permute-start | bytes 196616 | tf_op jit(solution)/shard_map/ppermute | solution.py:25
  20.5 6.6 %collective-permute-start.3 = (bf16[4,64,128]{2,1,0:T(8,128)(2,1)S(1)}, bf16[4,64,128]{2,1,0:T(8,128)(2,1)S(1)}, u32[]{:S(2)}, u32[]{:S(2)}) collective-permute-start(bf16[4,64,128]{2,1,0:T(8,128)(2,1)S(1)} %get-tuple-element.28), channel_id=1, source_target_pairs={{4,0},{5,1},{6,2},{7,3},{0,4},{1,5},{2,6},{3,7},{12,8},{13,9},{14,... | collective-permute-start | bytes 196616 | tf_op jit(solution)/shard_map/ppermute | solution.py:25
  20.5 6.6 %collective-permute-start.2 = (bf16[4,64,128]{2,1,0:T(8,128)(2,1)S(1)}, bf16[4,64,128]{2,1,0:T(8,128)(2,1)S(1)}, u32[]{:S(2)}, u32[]{:S(2)}) collective-permute-start(bf16[4,64,128]{2,1,0:T(8,128)(2,1)S(1)} %get-tuple-element.29), channel_id=1, source_target_pairs={{3,0},{4,1},{5,2},{6,3},{7,4},{0,5},{1,6},{2,7},{11,8},{12,9},{13,... | collective-permute-start | bytes 196616 | tf_op jit(solution)/shard_map/ppermute | solution.py:25
  20.5 6.6 %collective-permute-start.1 = (bf16[4,64,128]{2,1,0:T(8,128)(2,1)S(1)}, bf16[4,64,128]{2,1,0:T(8,128)(2,1)S(1)}, u32[]{:S(2)}, u32[]{:S(2)}) collective-permute-start(bf16[4,64,128]{2,1,0:T(8,128)(2,1)S(1)} %get-tuple-element.30), channel_id=1, source_target_pairs={{2,0},{3,1},{4,2},{5,3},{6,4},{7,5},{0,6},{1,7},{10,8},{11,9},{12,... | collective-permute-start | bytes 196616 | tf_op jit(solution)/shard_map/ppermute | solution.py:25
  39.0 7.4 %copy-start.3 = (f32[256,128]{1,0:T(8,128)S(1)}, f32[256,128]{1,0:T(8,128)}, u32[]{:S(2)}) copy-start(f32[256,128]{1,0:T(8,128)} %param.9) | copy-start | bytes 393220
  46.4 141.6 %all-gather.5.cloned.1.call-start = ((), (), s32[]{:S(2)}) async-start(), calls=%async_computation.3 | async-start | bytes 1310720 | tf_op jit(solution)/shard_map/all_gather | solution.py:144
  100.3 25.5 %collective-permute-start.4 = (f32[8,4,64,128]{3,2,1,0:T(8,128)S(1)}, f32[8,4,64,128]{3,2,1,0:T(8,128)S(1)}, u32[]{:S(2)}, u32[]{:S(2)}) collective-permute-start(f32[8,4,64,128]{3,2,1,0:T(8,128)S(1)} %bitcast.104), channel_id=1, source_target_pairs={{0,8},{8,0},{16,24},{24,16},{1,9},{9,1},{17,25},{25,17},{2,10},{10... | collective-permute-start | bytes 3145736 | tf_op jit(solution)/shard_map/ppermute | solution.py:15
  126.0 24.6 %collective-permute-start.5 = (f32[8,4,64,128]{3,2,1,0:T(8,128)S(1)}, f32[8,4,64,128]{3,2,1,0:T(8,128)S(1)}, u32[]{:S(2)}, u32[]{:S(2)}) collective-permute-start(f32[8,4,64,128]{3,2,1,0:T(8,128)S(1)} %add.161), channel_id=1, source_target_pairs={{0,16},{8,24},{16,0},{24,8},{1,17},{9,25},{17,1},{25,9},{2,18},{10... | collective-permute-start | bytes 3145736 | tf_op jit(solution)/shard_map/ppermute | solution.py:15
  151.3 5.6 %collective-permute-start.6 = (bf16[4,64,128]{2,1,0:T(8,128)(2,1)S(1)}, bf16[4,64,128]{2,1,0:T(8,128)(2,1)S(1)}, u32[]{:S(2)}, u32[]{:S(2)}) collective-permute-start(bf16[4,64,128]{2,1,0:T(8,128)(2,1)S(1)} %get-tuple-element.23), channel_id=1, source_target_pairs={{7,0},{0,1},{1,2},{2,3},{3,4},{4,5},{5,6},{6,7},{15,8},{8,9},{9,10... | collective-permute-start | bytes 196616 | tf_op jit(solution)/shard_map/ppermute | solution.py:25
  151.4 10.1 %collective-permute-start.9 = (bf16[4,64,128]{2,1,0:T(8,128)(2,1)S(1)}, bf16[4,64,128]{2,1,0:T(8,128)(2,1)S(1)}, u32[]{:S(2)}, u32[]{:S(2)}) collective-permute-start(bf16[4,64,128]{2,1,0:T(8,128)(2,1)S(1)} %get-tuple-element.24), channel_id=1, source_target_pairs={{4,0},{5,1},{6,2},{7,3},{0,4},{1,5},{2,6},{3,7},{12,8},{13,9},{14,... | collective-permute-start | bytes 196616 | tf_op jit(solution)/shard_map/ppermute | solution.py:25
  152.1 9.4 %collective-permute-start.8 = (bf16[4,64,128]{2,1,0:T(8,128)(2,1)S(1)}, bf16[4,64,128]{2,1,0:T(8,128)(2,1)S(1)}, u32[]{:S(2)}, u32[]{:S(2)}) collective-permute-start(bf16[4,64,128]{2,1,0:T(8,128)(2,1)S(1)} %get-tuple-element.25), channel_id=1, source_target_pairs={{5,0},{6,1},{7,2},{0,3},{1,4},{2,5},{3,6},{4,7},{13,8},{14,9},{15,... | collective-permute-start | bytes 196616 | tf_op jit(solution)/shard_map/ppermute | solution.py:25
  155.2 6.3 %collective-permute-start.7 = (bf16[4,64,128]{2,1,0:T(8,128)(2,1)S(1)}, bf16[4,64,128]{2,1,0:T(8,128)(2,1)S(1)}, u32[]{:S(2)}, u32[]{:S(2)}) collective-permute-start(bf16[4,64,128]{2,1,0:T(8,128)(2,1)S(1)} %get-tuple-element.26), channel_id=1, source_target_pairs={{6,0},{7,1},{0,2},{1,3},{2,4},{3,5},{4,6},{5,7},{14,8},{15,9},{8,1... | collective-permute-start | bytes 196616 | tf_op jit(solution)/shard_map/ppermute | solution.py:25
  163.0 99.8 %reduce-scatter.5.cloned.1.call-start = ((), (), s32[]{:S(2)}) async-start(), calls=%async_computation.4 | async-start | bytes 1179648 | tf_op jit(solution)/shard_map/reduce_scatter | solution.py:118
  192.2 6.2 %copy-start = (f32[16,64,128]{2,1,0:T(8,128)S(1)}, f32[16,64,128]{2,1,0:T(8,128)}, u32[]{:S(2)}) copy-start(f32[16,64,128]{2,1,0:T(8,128)} %param.10) | copy-start | bytes 1572868
  192.2 6.2 %copy-start.1 = (f32[16,64,128]{2,1,0:T(8,128)S(1)}, f32[16,64,128]{2,1,0:T(8,128)}, u32[]{:S(2)}) copy-start(f32[16,64,128]{2,1,0:T(8,128)} %param.11) | copy-start | bytes 1572868
  192.2 6.2 %copy-start.4 = (f32[128]{0:T(128)S(1)}, f32[128]{0:T(128)}, u32[]{:S(2)}) copy-start(f32[128]{0:T(128)} %param.13) | copy-start | bytes 1540
  200.9 6.2 %collective-permute-start.10 = (bf16[4,64,128]{2,1,0:T(8,128)(2,1)S(1)}, bf16[4,64,128]{2,1,0:T(8,128)(2,1)S(1)}, u32[]{:S(2)}, u32[]{:S(2)}) collective-permute-start(bf16[4,64,128]{2,1,0:T(8,128)(2,1)S(1)} %get-tuple-element.19), channel_id=1, source_target_pairs={{1,0},{2,1},{3,2},{4,3},{5,4},{6,5},{7,6},{0,7},{9,8},{10,9},{11,1... | collective-permute-start | bytes 196616 | tf_op jit(solution)/shard_map/ppermute | solution.py:25
  203.6 6.6 %collective-permute-start.13 = (bf16[4,64,128]{2,1,0:T(8,128)(2,1)S(1)}, bf16[4,64,128]{2,1,0:T(8,128)(2,1)S(1)}, u32[]{:S(2)}, u32[]{:S(2)}) collective-permute-start(bf16[4,64,128]{2,1,0:T(8,128)(2,1)S(1)} %get-tuple-element.20), channel_id=1, source_target_pairs={{4,0},{5,1},{6,2},{7,3},{0,4},{1,5},{2,6},{3,7},{12,8},{13,9},{14,... | collective-permute-start | bytes 196616 | tf_op jit(solution)/shard_map/ppermute | solution.py:25
  203.6 6.6 %collective-permute-start.12 = (bf16[4,64,128]{2,1,0:T(8,128)(2,1)S(1)}, bf16[4,64,128]{2,1,0:T(8,128)(2,1)S(1)}, u32[]{:S(2)}, u32[]{:S(2)}) collective-permute-start(bf16[4,64,128]{2,1,0:T(8,128)(2,1)S(1)} %get-tuple-element.21), channel_id=1, source_target_pairs={{3,0},{4,1},{5,2},{6,3},{7,4},{0,5},{1,6},{2,7},{11,8},{12,9},{13,... | collective-permute-start | bytes 196616 | tf_op jit(solution)/shard_map/ppermute | solution.py:25
  203.8 6.4 %collective-permute-start.11 = (bf16[4,64,128]{2,1,0:T(8,128)(2,1)S(1)}, bf16[4,64,128]{2,1,0:T(8,128)(2,1)S(1)}, u32[]{:S(2)}, u32[]{:S(2)}) collective-permute-start(bf16[4,64,128]{2,1,0:T(8,128)(2,1)S(1)} %get-tuple-element.22), channel_id=1, source_target_pairs={{2,0},{3,1},{4,2},{5,3},{6,4},{7,5},{0,6},{1,7},{10,8},{11,9},{12,... | collective-permute-start | bytes 196616 | tf_op jit(solution)/shard_map/ppermute | solution.py:25
  229.7 143.8 %all-gather.7.cloned.1.call-start = ((), (), s32[]{:S(2)}) async-start(), calls=%async_computation.5 | async-start | bytes 1310720 | tf_op jit(solution)/shard_map/all_gather | solution.py:144
  285.9 25.5 %collective-permute-start.14 = (f32[8,4,64,128]{3,2,1,0:T(8,128)S(1)}, f32[8,4,64,128]{3,2,1,0:T(8,128)S(1)}, u32[]{:S(2)}, u32[]{:S(2)}) collective-permute-start(f32[8,4,64,128]{3,2,1,0:T(8,128)S(1)} %bitcast.106), channel_id=1, source_target_pairs={{0,8},{8,0},{16,24},{24,16},{1,9},{9,1},{17,25},{25,17},{2,10},{10... | collective-permute-start | bytes 3145736 | tf_op jit(solution)/shard_map/ppermute | solution.py:15
  311.6 24.6 %collective-permute-start.15 = (f32[8,4,64,128]{3,2,1,0:T(8,128)S(1)}, f32[8,4,64,128]{3,2,1,0:T(8,128)S(1)}, u32[]{:S(2)}, u32[]{:S(2)}) collective-permute-start(f32[8,4,64,128]{3,2,1,0:T(8,128)S(1)} %add.170), channel_id=1, source_target_pairs={{0,16},{8,24},{16,0},{24,8},{1,17},{9,25},{17,1},{25,9},{2,18},{10... | collective-permute-start | bytes 3145736 | tf_op jit(solution)/shard_map/ppermute | solution.py:15
  337.0 5.6 %collective-permute-start.16 = (bf16[4,64,128]{2,1,0:T(8,128)(2,1)S(1)}, bf16[4,64,128]{2,1,0:T(8,128)(2,1)S(1)}, u32[]{:S(2)}, u32[]{:S(2)}) collective-permute-start(bf16[4,64,128]{2,1,0:T(8,128)(2,1)S(1)} %get-tuple-element.15), channel_id=1, source_target_pairs={{7,0},{0,1},{1,2},{2,3},{3,4},{4,5},{5,6},{6,7},{15,8},{8,9},{9,10... | collective-permute-start | bytes 196616 | tf_op jit(solution)/shard_map/ppermute | solution.py:25
  337.0 10.1 %collective-permute-start.19 = (bf16[4,64,128]{2,1,0:T(8,128)(2,1)S(1)}, bf16[4,64,128]{2,1,0:T(8,128)(2,1)S(1)}, u32[]{:S(2)}, u32[]{:S(2)}) collective-permute-start(bf16[4,64,128]{2,1,0:T(8,128)(2,1)S(1)} %get-tuple-element.16), channel_id=1, source_target_pairs={{4,0},{5,1},{6,2},{7,3},{0,4},{1,5},{2,6},{3,7},{12,8},{13,9},{14,... | collective-permute-start | bytes 196616 | tf_op jit(solution)/shard_map/ppermute | solution.py:25
  337.7 9.4 %collective-permute-start.18 = (bf16[4,64,128]{2,1,0:T(8,128)(2,1)S(1)}, bf16[4,64,128]{2,1,0:T(8,128)(2,1)S(1)}, u32[]{:S(2)}, u32[]{:S(2)}) collective-permute-start(bf16[4,64,128]{2,1,0:T(8,128)(2,1)S(1)} %get-tuple-element.17), channel_id=1, source_target_pairs={{5,0},{6,1},{7,2},{0,3},{1,4},{2,5},{3,6},{4,7},{13,8},{14,9},{15,... | collective-permute-start | bytes 196616 | tf_op jit(solution)/shard_map/ppermute | solution.py:25
  340.8 6.3 %collective-permute-start.17 = (bf16[4,64,128]{2,1,0:T(8,128)(2,1)S(1)}, bf16[4,64,128]{2,1,0:T(8,128)(2,1)S(1)}, u32[]{:S(2)}, u32[]{:S(2)}) collective-permute-start(bf16[4,64,128]{2,1,0:T(8,128)(2,1)S(1)} %get-tuple-element.18), channel_id=1, source_target_pairs={{6,0},{7,1},{0,2},{1,3},{2,4},{3,5},{4,6},{5,7},{14,8},{15,9},{8,1... | collective-permute-start | bytes 196616 | tf_op jit(solution)/shard_map/ppermute | solution.py:25
  377.7 6.1 %copy-start.2 = (f32[16,64,128]{2,1,0:T(8,128)S(1)}, f32[16,64,128]{2,1,0:T(8,128)}, u32[]{:S(2)}) copy-start(f32[16,64,128]{2,1,0:T(8,128)} %get-tuple-element.36) | copy-start | bytes 1572868
Sparse Core Ops, SparseCore 0:
  46.5 32.8 reduce-scatter.2
  163.1 24.7 all-gather.4
  229.8 32.9 reduce-scatter.4
  348.8 24.7 all-gather.6
